TPU v7x, 256 devices: a whole 4x4x8 slice. The times are simulated.
256 devices in a mesh: row: 8 (over z_hi, x), col: 32 (over y, z_lo, core).
Axes of the slice: x: 4, y: 4, z: 8 (z_hi: 2, z_lo: 4; z = z_hi * 4 + z_lo), core: 2. Of those that a mesh axis runs over, the one named last changes fastest.
Arguments:
- inv_anc: float32 [8, 32, 48, 12288], P(None, 'col', None, 'row'), may hold values from -6 to 6
- factor_cols: float32 [4, 12288, 256], P(None, ('row', 'col')), may hold values from -0.0546875 to 0.0546875
- couple: float32 [6, 256, 256], replicated, may hold values from -0.1875 to 0.1875
- diag_inv: float32 [4, 256, 256], replicated, may hold values from -6 to 6, as said below
- pattern: int32 [4, 48], replicated, may hold values 0 or 1
- parent: int32 [4], replicated, may hold values from 0 to 4, as said below
Outputs:
- inv_cols: float32 [4, 12288, 256], P(None, ('row', 'col'))
- win_cols: float32 [6, 256, 256], replicated
- win_diag: float32 [4, 256, 256], replicated
Inputs may be any that keep to these rules, and one draw needn't show every extreme that they name: parent[0] is 4, meaning a parent in the ancestor set; for j of 1 or more parent[j] is an earlier supernode or 4. Each diag_inv[j] is symmetric.
All inputs are finite; a program needn't handle non-finite values.
Results may differ from a plain program's by a relative error of at most 0.0001.
Values sent between devices are 32-bit elements; how exact they have to be, the bound alone decides.
No kernel may reach another device: no remote copies, remote signals or barrier semaphores. Data moves between devices by JAX's collectives and lax.ppermute only.
A program may use at most 64 MiB of HBM per device.

v0:
```python
import functools

import jax
import jax.numpy as jnp
from jax import lax
from jax.experimental import pallas as pl
from jax.experimental.pallas import tpu as pltpu
from jax.sharding import PartitionSpec as P


W = 256
NSUP = 4
RW = 48
HALF = W // 2
SIZES = {"zh": 2, "x": 4, "y": 4, "zl": 4, "c": 2}
BOTH = ("row", "col")
F32, BF16 = jnp.float32, jnp.bfloat16
PAIRS = [(m, j) for j in range(NSUP) for m in range(j)]
ALL_BLOCKS = PAIRS + [(j, j) for j in range(NSUP)]
DIAG = len(PAIRS) * W
TALL = DIAG + 3 * W
VMEM = pl.BlockSpec(memory_space=pltpu.VMEM)
SMEM = pl.BlockSpec(memory_space=pltpu.SMEM)


def place():
    row, col = lax.axis_index("row"), lax.axis_index("col")
    return {"zh": row >> 2, "x": row & 3, "y": col >> 3, "zl": (col >> 1) & 3, "c": col & 1}


def moved(value, axis, step):
    return sent(value, axis, lambda a: (a + step) % SIZES[axis])


def sent(value, axis, rule):
    names = list(SIZES)
    perm = []
    for device in range(256):
        rest, at = device, {}
        for name in reversed(names):
            at[name] = rest % SIZES[name]
            rest //= SIZES[name]
        at[axis] = rule(at[axis])
        target = 0
        for name in names:
            target = target * SIZES[name] + at[name]
        perm.append((device, target))
    return lax.ppermute(value, BOTH, perm)


def tie(*values):
    return lax.optimization_barrier(values)


def halves(value):
    top = value.astype(BF16)
    return top, (value - top.astype(F32)).astype(BF16)


def mul(left, right, over=(1, 0)):
    dims = (((over[0],), (over[1],)), ((), ()))
    dot = lambda u, v: lax.dot_general(u, v, dims, preferred_element_type=F32)
    return dot(left[0], right[0]) + (dot(left[1], right[0]) + dot(left[0], right[1]))


def couplings(couple, parent):
    linked = {}
    blocks = {}
    for j in range(NSUP):
        for m in range(j):
            now = parent[j] == m
            for p in range(m + 1, j):
                now = now | ((parent[j] == p) & linked[p, m])
            linked[j, m] = now
            blocks[j, m] = couple[j * (j - 1) // 2 + m] * jnp.where(now, 1.0, 0.0).astype(F32)
    return blocks


def pre_kernel(parent, pattern, factor, couple, out):
    first = (lax.axis_index("row") * 32 + lax.axis_index("col")) * RW
    block = first >> 8
    after = jnp.minimum(block + 1, pattern.shape[1] - 1)
    edge = (block + 1) * W - first
    low = lax.broadcasted_iota(jnp.int32, (RW, W), 0) < edge
    blocks = couplings(couple, parent)
    values = []
    for j in range(NSUP):
        here, there = pattern[j, block].astype(F32), pattern[j, after].astype(F32)
        values.append(factor[j] * jnp.where(low, here, there))
    for m in range(NSUP):
        out[:, m * W : (m + 1) * W] = values[m]
        left = halves(values[m])
        for j in range(m + 1, NSUP):
            values[j] = values[j] - mul(left, halves(blocks[j, m]))


def base_table(order):
    at = lambda q, j: order.index((q, j))
    return [(at(m, j), at(q, m), at(q, j)) for j in range(NSUP) for m in range(j + 1) for q in range(m)]


def base_kernel(order, parent, table, couple, diag_inv, out, *held):
    chigh, clow, ihigh, ilow, shigh, slow = held
    at = lambda q, j: order.index((q, j))

    def keep(high, low, i, value):
        high[i], low[i] = halves(value)

    def kept(high, low, i):
        return high[i], low[i]

    for (j, m), value in couplings(couple, parent).items():
        keep(chigh, clow, at(m, j), value)
        keep(ihigh, ilow, at(m, j), -value)
    for gap in range(2, NSUP):
        for m in range(NSUP - gap):
            j = m + gap
            value = -(chigh[at(m, j)].astype(F32) + clow[at(m, j)].astype(F32))
            for q in range(m + 1, j):
                value = value - mul(kept(ihigh, ilow, at(m, q)), kept(chigh, clow, at(q, j)))
            keep(ihigh, ilow, at(m, j), value)
    for q in range(NSUP):
        out[at(q, q) * W : (at(q, q) + 1) * W, :] = diag_inv[q]
        keep(shigh, slow, at(q, q), diag_inv[q])
        for j in range(q + 1, NSUP):
            i = at(q, j)
            value = mul(kept(shigh, slow, at(q, q)), kept(ihigh, ilow, i))
            out[i * W : (i + 1) * W, :] = value
            keep(shigh, slow, i, value)

    def gain(t, carry):
        where = pl.ds(pl.multiple_of(table[t, 0] * W, W), W)
        left, right = kept(ihigh, ilow, table[t, 1]), kept(shigh, slow, table[t, 2])
        out[where, :] = out[where, :] + mul(left, right, (0, 0))
        return carry

    lax.fori_loop(0, len(base_table(order)), gain, 0)


def put(piece, top, bot, row_of, weight=None):
    def step(r, carry):
        src = pl.multiple_of(r * RW, 16)
        dst = pl.multiple_of(row_of(r), 16)
        value = piece[pl.ds(src, RW), :]
        hi, lo = halves(value if weight is None else value * weight(r))
        top[pl.ds(dst, RW), :] = hi
        bot[pl.ds(dst, RW), :] = lo
        return carry

    lax.fori_loop(0, piece.shape[0] // RW, step, 0)


def near_kernel(local, own, rest, twin, cross, out, ltop, lbot, rtop, rbot, top, bot):
    at = place()
    span = local.shape[1] // 4
    for i, k in enumerate((0, 1, 3, 2)):
        src = pl.multiple_of(((at["y"] - k) & 3) * span, 128)

        def step(t, carry, src=src, i=i):
            rows = pl.ds(pl.multiple_of(t * RW, 16), RW)
            hi, lo = halves(local[rows, pl.ds(src, span)])
            ltop[rows, i * span : (i + 1) * span] = hi
            lbot[rows, i * span : (i + 1) * span] = lo
            return carry

        lax.fori_loop(0, local.shape[0] // RW, step, 0)
    put(cross, rtop, rbot, lambda r: r * RW, lambda r: jnp.where(r == 1, 1.0, 0.5).astype(F32))
    for piece, par, skip in ((own, 0, 0), (rest, 0, 1), (twin, 1, 0)):
        core = at["c"] ^ par
        put(piece, top, bot, lambda r: (((at["zl"] - r - skip) & 3) * 2 + core) * RW)
    out[...] = mul((ltop[:, :span], lbot[:, :span]), (top[...], bot[...]))


def early_kernel(start, ltop, lbot, *refs):
    pieces, (out, top, bot) = refs[:6], refs[6:]
    at = place()
    span = ltop.shape[1] // 4
    for i, piece in enumerate(pieces):
        core = at["c"] ^ (i // 3)
        if i % 3 == 0:
            put(piece, top, bot, lambda r: (r * 8 + at["zl"] * 2 + core) * RW)
        else:
            side = i % 3 - 1
            put(piece, top, bot, lambda r: (side * 8 + ((at["zl"] - r - 1) & 3) * 2 + core) * RW)
    cols = slice(span, 3 * span)
    out[...] = start[...] + mul((ltop[:, cols], lbot[:, cols]), (top[...], bot[...]))


def main_kernel(*refs):
    early, ltop, lbot, ra, rb, distant = refs[:6]
    pieces, outs = refs[6:10], refs[10:14]
    kept, given = refs[14], refs[15]
    top, bot, rtop, rbot, result, ptop, pbot = refs[16:]
    at = place()
    span = ltop.shape[1] // 4
    quad = ra.shape[0]
    for i, piece in enumerate(pieces):
        core = at["c"] ^ (i // 2)
        start = 2 * (i % 2)
        put(piece, top, bot, lambda r: (((at["zl"] - r - start) & 3) * 2 + core) * RW)
    rtop[:quad, :] = ra[...]
    rbot[:quad, :] = rb[...]
    put(distant, rtop, rbot, lambda r: quad + r * RW)
    cols = slice(3 * span, 4 * span)
    value = early[...] + mul((ltop[:, cols], lbot[:, cols]), (top[...], bot[...]))
    result[...] = value
    taken = [at["zh"] * 4 + ((at["x"] + k) & 3) for k in range(3)]
    taken += [(1 - at["zh"]) * 4 + ((at["x"] + k + at["zh"]) & 3) for k in range(2)]
    for i, block in enumerate(taken):
        hi, lo = halves(result[pl.ds(pl.multiple_of(block * RW, 16), RW), :])
        ptop[i * RW : (i + 1) * RW, :] = hi
        pbot[i * RW : (i + 1) * RW, :] = lo
    for k, out in enumerate(outs):
        xa = (at["x"] + k) & 3
        for r in range(2):
            out[r] = result[pl.ds(pl.multiple_of((r * 4 + xa) * RW, 16), RW), :]
    even = at["c"] == 0

    def share(row, zero, one):
        rows = slice(row, row + zero.shape[0])
        kept[rows, :] = jnp.where(even, zero, one)
        given[rows, :] = jnp.where(even, one, zero)

    def factors(s):
        cols = slice(s * W, (s + 1) * W)
        return (rtop[:, cols], rbot[:, cols]), (ptop[:, cols], pbot[:, cols])

    for i, (m, j) in enumerate(PAIRS):
        (row_m, part_m), (row_j, part_j) = factors(m), factors(j)
        block = mul(row_m, part_j, (0, 0)) + mul(part_m, row_j, (0, 0))
        share(i * W, block[:, :HALF], block[:, HALF:])
    for t in range(2):
        here, there = (mul(*factors(s), (0, 0)) for s in (t, t + 2))
        here, there = here + here.T, there + there.T
        share(DIAG + t * W, here[:, :HALF], there[:, HALF:])
        share(DIAG + 2 * W + t * HALF, there[:HALF, :HALF], here[HALF:, HALF:])


def pick_kernel(*refs):
    pieces, keep, give = refs[:4], refs[4], refs[5]
    zh = place()["zh"]
    for out, side in ((keep, zh), (give, 1 - zh)):
        total = pieces[0][side]
        for piece in pieces[1:]:
            total = total + piece[side]
        out[...] = total


def final_kernel(*refs):
    pieces, (keep, got, base) = refs[:8], refs[8:11]
    columns, pair_out, diag_out, whole = refs[11:]
    at = place()
    rows = pieces[0].shape[0]
    small = rows // 4
    for i, piece in enumerate(pieces):
        par, k = divmod(i, 4)
        for r in range(4):
            dst = pl.multiple_of(((at["y"] - k) & 3) * rows + ((at["x"] - r) & 3) * small, 8)
            whole[at["c"] ^ par, pl.ds(dst, small), :] = piece[r * small : (r + 1) * small, :]
    left, right = slice(0, HALF), slice(HALF, W)
    for p in range(len(PAIRS)):
        span = slice(p * W, (p + 1) * W)
        pair_out[p, :, left] = whole[0, span, :] + base[span, left]
        pair_out[p, :, right] = whole[1, span, :] + base[span, right]
    for t in range(2):
        full = slice(DIAG + t * W, DIAG + (t + 1) * W)
        quarter = slice(DIAG + 2 * W + t * HALF, DIAG + 2 * W + (t + 1) * HALF)
        upper, lower = (base.at[DIAG + s * W : DIAG + (s + 1) * W, :] for s in (t, t + 2))
        side = whole[0, full, :]
        diag_out[t, :, left] = side + upper[:, left]
        diag_out[t, :HALF, right] = side[HALF:, :].T + upper[:HALF, right]
        diag_out[t, HALF:, right] = whole[1, quarter, :] + upper[HALF:, right]
        side = whole[1, full, :]
        diag_out[t + 2, :, right] = side + lower[:, right]
        diag_out[t + 2, HALF:, left] = side[:HALF, :].T + lower[HALF:, left]
        diag_out[t + 2, :HALF, left] = whole[0, quarter, :] + lower[:HALF, left]
    for j in range(NSUP):
        cols = slice(j * W, (j + 1) * W)
        columns[j] = -(keep[:, cols] + got[:, cols])


def kernel(body, args, out_shapes, scratch=(), smem=0, flops=0):
    single = not isinstance(out_shapes, list)
    return pl.pallas_call(
        body,
        out_shape=jax.ShapeDtypeStruct(out_shapes, F32)
        if single
        else [jax.ShapeDtypeStruct(s, F32) if isinstance(s[-1], int) else jax.ShapeDtypeStruct(*s) for s in out_shapes],
        in_specs=[SMEM] * smem + [VMEM] * (len(args) - smem),
        out_specs=VMEM if single else [VMEM] * len(out_shapes),
        scratch_shapes=[pltpu.VMEM(s, t) for s, t in scratch],
        compiler_params=pltpu.CompilerParams(vmem_limit_bytes=56 << 20),
        cost_estimate=pl.CostEstimate(
            flops=flops, transcendentals=0, bytes_accessed=sum(4 * a.size for a in args)
        ),
    )(*args)


def split_sum(values, at, axis):
    n = SIZES[axis]
    rows = values[0].shape[0] // n
    part = lambda v, k: lax.dynamic_slice_in_dim(v, ((at[axis] + k) & (n - 1)) * rows, rows, 0)
    return [total_of([part(v, k) for v in values]) for k in range(n)]


def scattered(pieces, axis):
    return [pieces[0]] + [moved(pieces[k], axis, k) for k in range(1, len(pieces))]


def gathered(value, axis):
    return [value] + [moved(value, axis, k) for k in range(1, SIZES[axis])]


def total_of(values):
    total = values[0]
    for value in values[1:]:
        total = total + value
    return total


def shards(inv_anc, factor_cols, couple, diag_inv, pattern, parent):
    at = place()
    local = inv_anc.reshape(-1, inv_anc.shape[3])
    height = local.shape[0]

    own = kernel(
        pre_kernel, [parent, pattern, factor_cols, couple], (RW, NSUP * W), smem=2, flops=1 << 20
    )
    width = NSUP * W
    tall = len(ALL_BLOCKS) * W
    span = local.shape[1] // 4

    near = gathered(own, "zl")
    firsts = [moved(own, "y", 1), moved(own, "y", 3)]
    cross = [own, moved(own, "x", 3), moved(own, "x", 2)]
    _, couple_later = tie(own, couple)
    base = kernel(
        functools.partial(base_kernel, ALL_BLOCKS),
        [parent, jnp.array(base_table(ALL_BLOCKS), jnp.int32), couple_later, diag_inv],
        (tall, W),
        [((len(ALL_BLOCKS), W, W), BF16)] * 6,
        smem=2,
        flops=1 << 31,
    )
    rest = jnp.concatenate(near[1:], axis=0)
    both = jnp.concatenate(firsts, axis=0)
    cross, both = tie(jnp.concatenate(cross, axis=0), both)

    left, right = moved(rest, "y", 1), moved(rest, "y", 3)
    distant = moved(lax.dynamic_slice_in_dim(cross, (1 - at["zh"]) * RW, 2 * RW, 0), "zh", 1)
    twin = moved(jnp.concatenate([own, rest], axis=0), "c", 1)
    start, ltop, lbot, ra, rb = kernel(
        near_kernel,
        [local, own, rest, twin, cross],
        [(height, width)] + [((height, 4 * span), BF16)] * 2 + [(cross.shape, BF16)] * 2,
        [((span, width), BF16)] * 2,
        flops=1 << 31,
    )
    left, right, start = tie(left, right, start)
    far_a = moved(jnp.concatenate([firsts[0], left[:RW]], axis=0), "y", 1)
    far_b = moved(right[RW:], "y", 3)
    both2 = moved(both, "c", 1)
    left2, right2 = moved(left, "c", 1), moved(right, "c", 1)
    early = kernel(
        early_kernel,
        [start, ltop, lbot, both, left, right, both2, left2, right2],
        (height, width),
        [((2 * span, width), BF16)] * 2,
        flops=1 << 31,
    )
    far_a, far_b, early = tie(far_a, far_b, early)
    *parts, kept, given = kernel(
        main_kernel,
        [early, ltop, lbot, ra, rb, distant]
        + [far_a, far_b, moved(far_a, "c", 1), moved(far_b, "c", 1)],
        [(2, RW, width)] * 4 + [(TALL, HALF)] * 2,
        [((span, width), BF16)] * 2
        + [((5 * RW, width), BF16)] * 2
        + [((height, width), F32)]
        + [((5 * RW, width), BF16)] * 2,
        flops=1 << 32,
    )

    got = moved(given, "c", 1)
    cut = split_sum([kept, got], at, "y")
    cols = scattered(parts, "x")
    across = scattered(cut, "y")
    keep, give = kernel(pick_kernel, cols, [(RW, width)] * 2)
    summed = moved(give, "zh", 1)
    cut = split_sum(across, at, "x")
    total = total_of(scattered(cut, "x"))
    total = total + sent(total, "zl", lambda a: a ^ 1)
    total = total + sent(total, "zl", lambda a: a ^ 2)
    total = total + moved(total, "zh", 1)
    lines = gathered(total, "x")
    total = jnp.concatenate(lines, axis=0)
    lanes = gathered(total, "y")
    twins = [moved(v, "c", 1) for v in lanes]
    return kernel(
        final_kernel,
        lanes + twins + [keep, summed, base],
        [(NSUP, RW, W), (len(PAIRS), W, W), (NSUP, W, W)],
        [((2, TALL, HALF), F32)],
    )


def solution(mesh):
    in_specs = (P(None, "col", None, "row"), P(None, BOTH, None), P(), P(), P(), P())
    out_specs = (P(None, BOTH, None), P(), P())

    return jax.shard_map(shards, mesh=mesh, in_specs=in_specs, out_specs=out_specs, check_vma=False)
```

profile of v0, /device:TPU:65, one launch (start us, length us, event | category | flops | bytes accessed | tf_op | source)
XLA Modules:
  0.0 190.6 jit_solution(6928785174896403757)
XLA Ops:
  3.5 3.7 %collective-permute-start.2 = (f32[48,1024]{1,0:T(8,128)}, f32[48,1024]{1,0:T(8,128)S(1)}, u32[]{:S(2)}, u32[]{:S(2)}) collective-permute-start(f32[48,1024]{1,0:T(8,128)} %shard_map.94.own), channel_id=1, source_target_pairs={{0,4},{1,5},{2,6},{3,7},{4,0},{5,1},{6,2},{7,3},{8,12},{9,13},{10,... | collective-permute-start | bytes 589832 | tf_op jit(solution)/shard_map/ppermute | solution.py:48
  10.0 10.6 %collective-permute-done.2 = f32[48,1024]{1,0:T(8,128)S(1)} collective-permute-done((f32[48,1024]{1,0:T(8,128)}, f32[48,1024]{1,0:T(8,128)S(1)}, u32[]{:S(2)}, u32[]{:S(2)}) %collective-permute-start.2) | collective-permute-done | bytes 196640 | tf_op jit(solution)/shard_map/ppermute | solution.py:48
  20.6 3.1 %collective-permute-done.1 = f32[48,1024]{1,0:T(8,128)S(1)} collective-permute-done((f32[48,1024]{1,0:T(8,128)}, f32[48,1024]{1,0:T(8,128)S(1)}, u32[]{:S(2)}, u32[]{:S(2)}) %collective-permute-start.1) | collective-permute-done | bytes 196640 | tf_op jit(solution)/shard_map/ppermute | solution.py:48
  39.5 4.3 %collective-permute-done.7 = f32[48,1024]{1,0:T(8,128)S(1)} collective-permute-done((f32[48,1024]{1,0:T(8,128)S(1)}, f32[48,1024]{1,0:T(8,128)S(1)}, u32[]{:S(2)}, u32[]{:S(2)}) %collective-permute-start.7) | collective-permute-done | bytes 196640 | tf_op jit(solution)/shard_map/ppermute | solution.py:48
  45.5 5.7 %shard_map.95 = (f32[384,1024]{1,0:T(8,128)}, bf16[384,1536]{1,0:T(8,128)(2,1)}, bf16[384,1536]{1,0:T(8,128)(2,1)}, bf16[144,1024]{1,0:T(8,128)(2,1)}, bf16[144,1024]{1,0:T(8,128)(2,1)}) custom-call(f32[384,1536]{1,0:T(8,128)} %bitcast.1, f32[48,1024]{1,0:T(8,128)} %shard_map.94.own, f32[144,1024]{1,0:T(8,128)} %copy-done.19, f32[192,1024]{1,0:T(8,128)} %copy-done.20, ...), custom_call_target="tpu_custom_call" | custom-call | flops 2147483648 | bytes 4521984 | tf_op jit(solution)/shard_map/pallas_call | solution.py:284
  55.1 3.4 %collective-permute-start.11 = (f32[96,1024]{1,0:T(8,128)}, f32[96,1024]{1,0:T(8,128)}, u32[]{:S(2)}, u32[]{:S(2)}) collective-permute-start(f32[96,1024]{1,0:T(8,128)} %slice.7), channel_id=1, source_target_pairs={{0,24},{1,25},{2,26},{3,27},{4,28},{5,29},{6,30},{7,31},{8,0},{9,1... | collective-permute-start | bytes 1179656 | tf_op jit(solution)/shard_map/ppermute | solution.py:48
  59.3 5.2 %collective-permute-start.15 = (f32[96,1024]{1,0:T(8,128)S(1)}, f32[96,1024]{1,0:T(8,128)S(1)}, u32[]{:S(2)}, u32[]{:S(2)}) collective-permute-start(f32[96,1024]{1,0:T(8,128)S(1)} %constant_dynamic-slice_fusion), channel_id=1, source_target_pairs={{0,128},{1,129},{2,130},{3,131},{4,132},{5,133},{6,134},{7,135},{8... | collective-permute-start | bytes 1179656 | tf_op jit(solution)/shard_map/ppermute | solution.py:48
  65.7 6.7 %shard_map.96.refs_0_ = f32[384,1024]{1,0:T(8,128)} custom-call(f32[384,1024]{1,0:T(8,128)} %get-tuple-element.29.start, bf16[384,1536]{1,0:T(8,128)(2,1)} %get-tuple-element.30.ltop.refs_1_, bf16[384,1536]{1,0:T(8,128)(2,1)} %get-tuple-element.31.lbot.refs_2_, f32[96,1024]{1,0:T(8,128)} %copy-done.3, f32[144,1024]{1,0:T(8,128)} %copy-done.5, ...), custom_call_target="tpu_custom_call" | custom-call | flops 2147483648 | bytes 9437184 | tf_op jit(solution)/shard_map/pallas_call | solution.py:284
  73.2 9.5 %collective-permute-done.15.refs_5_ = f32[96,1024]{1,0:T(8,128)S(1)} collective-permute-done((f32[96,1024]{1,0:T(8,128)S(1)}, f32[96,1024]{1,0:T(8,128)S(1)}, u32[]{:S(2)}, u32[]{:S(2)}) %collective-permute-start.15) | collective-permute-done | bytes 393248 | tf_op jit(solution)/shard_map/ppermute | solution.py:48
  83.7 8.1 %shard_map.97 = (f32[2,48,1024]{2,1,0:T(8,128)}, f32[2,48,1024]{2,1,0:T(8,128)}, f32[2,48,1024]{2,1,0:T(8,128)}, f32[2,48,1024]{2,1,0:T(8,128)}, f32[2304,128]{1,0:T(8,128)}, /*index=5*/f32[2304,128]{1,0:T(8,128)}) custom-call(f32[384,1024]{1,0:T(8,128)} %shard_map.96.refs_0_, bf16[384,1536]{1,0:T(8,128)(2,1)} %get-tuple-element.30.ltop.refs_1_, ...), custom_call_target="tpu_custom_call" | custom-call | flops 4294967296 | bytes 9437184 | tf_op jit(solution)/shard_map/pallas_call | solution.py:284
  99.9 11.5 %collective-permute-done.21 = f32[576,128]{1,0:T(8,128)S(1)} collective-permute-done((f32[576,128]{1,0:T(8,128)S(1)}, f32[576,128]{1,0:T(8,128)S(1)}, u32[]{:S(2)}, u32[]{:S(2)}) %collective-permute-start.21) | collective-permute-done | bytes 294944 | tf_op jit(solution)/shard_map/ppermute | solution.py:48
  111.4 4.0 %collective-permute-done.19 = f32[576,128]{1,0:T(8,128)S(1)} collective-permute-done((f32[576,128]{1,0:T(8,128)S(1)}, f32[576,128]{1,0:T(8,128)S(1)}, u32[]{:S(2)}, u32[]{:S(2)}) %collective-permute-start.19) | collective-permute-done | bytes 294944 | tf_op jit(solution)/shard_map/ppermute | solution.py:48
  119.9 3.0 %collective-permute-done.23 = f32[144,128]{1,0:T(8,128)S(1)} collective-permute-done((f32[144,128]{1,0:T(8,128)S(1)}, f32[144,128]{1,0:T(8,128)S(1)}, u32[]{:S(2)}, u32[]{:S(2)}) %collective-permute-start.23) | collective-permute-done | bytes 73760 | tf_op jit(solution)/shard_map/ppermute | solution.py:48
  126.6 4.4 %collective-permute-done.26 = f32[144,128]{1,0:T(8,128)S(1)} collective-permute-done((f32[144,128]{1,0:T(8,128)S(1)}, f32[144,128]{1,0:T(8,128)S(1)}, u32[]{:S(2)}, u32[]{:S(2)}) %collective-permute-start.26) | collective-permute-done | bytes 73760 | tf_op jit(solution)/shard_map/ppermute | solution.py:48
  131.0 5.1 %collective-permute-start.27 = (f32[144,128]{1,0:T(8,128)S(1)}, f32[144,128]{1,0:T(8,128)S(1)}, u32[]{:S(2)}, u32[]{:S(2)}) collective-permute-start(f32[144,128]{1,0:T(8,128)S(1)} %add.174), channel_id=1, source_target_pairs={{0,128},{1,129},{2,130},{3,131},{4,132},{5,133},{6,134},{7,135},{8... | collective-permute-start | bytes 221192 | tf_op jit(solution)/shard_map/ppermute | solution.py:48
  136.0 3.6 %collective-permute-done.27 = f32[144,128]{1,0:T(8,128)S(1)} collective-permute-done((f32[144,128]{1,0:T(8,128)S(1)}, f32[144,128]{1,0:T(8,128)S(1)}, u32[]{:S(2)}, u32[]{:S(2)}) %collective-permute-start.27) | collective-permute-done | bytes 73760 | tf_op jit(solution)/shard_map/ppermute | solution.py:48
  141.7 3.1 %collective-permute-start.39 = (f32[2,48,1024]{2,1,0:T(8,128)S(1)}, f32[2,48,1024]{2,1,0:T(8,128)S(1)}, u32[]{:S(2)}, u32[]{:S(2)}) collective-permute-start(f32[2,48,1024]{2,1,0:T(8,128)S(1)} %copy-done.22), channel_id=1, source_target_pairs={{0,64},{1,65},{2,66},{3,67},{4,68},{5,69},{6,70},{7,71},{8,72},{9,... | collective-permute-start | bytes 1179656 | tf_op jit(solution)/shard_map/ppermute | solution.py:48
  150.7 7.7 %collective-permute-start.34 = (f32[576,128]{1,0:T(8,128)S(1)}, f32[576,128]{1,0:T(8,128)S(1)}, u32[]{:S(2)}, u32[]{:S(2)}) collective-permute-start(f32[576,128]{1,0:T(8,128)S(1)} %pad_maximum_fusion.4.refs_0_), channel_id=1, source_target_pairs={{0,1},{1,0},{2,3},{3,2},{4,5},{5,4},{6,7},{7,6},{8,9},{9,8},{10,11... | collective-permute-start | bytes 884744 | tf_op jit(solution)/shard_map/ppermute | solution.py:48
  158.4 4.6 %collective-permute-start.37 = (f32[576,128]{1,0:T(8,128)S(1)}, f32[576,128]{1,0:T(8,128)S(1)}, u32[]{:S(2)}, u32[]{:S(2)}) collective-permute-start(f32[576,128]{1,0:T(8,128)S(1)} %collective-permute-done.33.refs_3_), channel_id=1, source_target_pairs={{0,1},{1,0},{2,3},{3,2},{4,5},{5,4},{6,7},{7,6},{8,9},{9,8},{10,11... | collective-permute-start | bytes 884744 | tf_op jit(solution)/shard_map/ppermute | solution.py:48
  164.8 3.1 %collective-permute-start.35 = (f32[576,128]{1,0:T(8,128)S(1)}, f32[576,128]{1,0:T(8,128)S(1)}, u32[]{:S(2)}, u32[]{:S(2)}) collective-permute-start(f32[576,128]{1,0:T(8,128)S(1)} %collective-permute-done.31.refs_1_), channel_id=1, source_target_pairs={{0,1},{1,0},{2,3},{3,2},{4,5},{5,4},{6,7},{7,6},{8,9},{9,8},{10,11... | collective-permute-start | bytes 884744 | tf_op jit(solution)/shard_map/ppermute | solution.py:48
  170.7 3.1 %collective-permute-start.41 = (f32[48,1024]{1,0:T(8,128)}, f32[48,1024]{1,0:T(8,128)S(1)}, u32[]{:S(2)}, u32[]{:S(2)}) collective-permute-start(f32[48,1024]{1,0:T(8,128)} %get-tuple-element.45), channel_id=1, source_target_pairs={{0,128},{1,129},{2,130},{3,131},{4,132},{5,133},{6,134},{7,135},{8... | collective-permute-start | bytes 589832 | tf_op jit(solution)/shard_map/ppermute | solution.py:48
  173.8 7.8 %shard_map.99.refs_10_ = f32[2560,256]{1,0:T(8,128)} custom-call(s32[4]{0:T(128)} %parent.3, s32[10,3]{1,0:T(8,128)} %constant.27.clone.table, f32[6,256,256]{2,1,0:T(8,128)} %couple.2, f32[4,256,256]{2,1,0:T(8,128)} %diag_inv.1), custom_call_target="tpu_custom_call" | custom-call | flops 2147483648 | bytes 2621576 | tf_op jit(solution)/shard_map/pallas_call | solution.py:284
  181.7 3.3 %collective-permute-done.41.refs_9_ = f32[48,1024]{1,0:T(8,128)S(1)} collective-permute-done((f32[48,1024]{1,0:T(8,128)}, f32[48,1024]{1,0:T(8,128)S(1)}, u32[]{:S(2)}, u32[]{:S(2)}) %collective-permute-start.41) | collective-permute-done | bytes 196640 | tf_op jit(solution)/shard_map/ppermute | solution.py:48
  186.1 4.5 %shard_map.100 = (f32[4,48,256]{2,1,0:T(8,128)}, f32[6,256,256]{2,1,0:T(8,128)}, f32[4,256,256]{2,1,0:T(8,128)}) custom-call(f32[576,128]{1,0:T(8,128)} %copy-done.4, f32[576,128]{1,0:T(8,128)} %copy-done.13, f32[576,128]{1,0:T(8,128)} %copy-done.12, f32[576,128]{1,0:T(8,128)} %copy-done.11, f32[576,128]{1,0:T(8,128)} %copy-done.14, f32[576,128]{1,0:T(8,128)} %copy-done.17, ...), custom_call_target="tpu_custom_call" | custom-call | bytes 5373952 | tf_op jit(solution)/shard_map/pallas_call | solution.py:284
  (138 shorter events, 60.7 us)
Async XLA Ops:
  3.5 17.1 %collective-permute-start.2 = (f32[48,1024]{1,0:T(8,128)}, f32[48,1024]{1,0:T(8,128)S(1)}, u32[]{:S(2)}, u32[]{:S(2)}) collective-permute-start(f32[48,1024]{1,0:T(8,128)} %shard_map.94.own), channel_id=1, source_target_pairs={{0,4},{1,5},{2,6},{3,7},{4,0},{5,1},{6,2},{7,3},{8,12},{9,13},{10,... | collective-permute-start | bytes 589832 | tf_op jit(solution)/shard_map/ppermute | solution.py:48
  7.2 16.5 %collective-permute-start.1 = (f32[48,1024]{1,0:T(8,128)}, f32[48,1024]{1,0:T(8,128)S(1)}, u32[]{:S(2)}, u32[]{:S(2)}) collective-permute-start(f32[48,1024]{1,0:T(8,128)} %shard_map.94.own), channel_id=1, source_target_pairs={{0,2},{1,3},{2,4},{3,5},{4,6},{5,7},{6,0},{7,1},{8,10},{9,11},{10,... | collective-permute-start | bytes 589832 | tf_op jit(solution)/shard_map/ppermute | solution.py:48
  24.6 20.0 %collective-permute-start.6 = (f32[192,1024]{1,0:T(8,128)S(1)}, f32[192,1024]{1,0:T(8,128)S(1)}, u32[]{:S(2)}, u32[]{:S(2)}) collective-permute-start(f32[192,1024]{1,0:T(8,128)S(1)} %pad_maximum_fusion), channel_id=1, source_target_pairs={{0,1},{1,0},{2,3},{3,2},{4,5},{5,4},{6,7},{7,6},{8,9},{9,8},{10,11... | collective-permute-start | bytes 2359304 | tf_op jit(solution)/shard_map/ppermute | solution.py:48
  28.9 22.3 %collective-permute-start.5 = (f32[144,1024]{1,0:T(8,128)S(1)}, f32[144,1024]{1,0:T(8,128)S(1)}, u32[]{:S(2)}, u32[]{:S(2)}) collective-permute-start(f32[144,1024]{1,0:T(8,128)S(1)} %constant_dynamic-update-slice_fusion.rest), channel_id=1, source_target_pairs={{0,24},{1,25},{2,26},{3,27},{4,28},{5,29},{6,30},{7,31},{8,0},{9,1... | collective-permute-start | bytes 1769480 | tf_op jit(solution)/shard_map/ppermute | solution.py:48
  31.7 19.6 %collective-permute-start.4 = (f32[144,1024]{1,0:T(8,128)S(1)}, f32[144,1024]{1,0:T(8,128)S(1)}, u32[]{:S(2)}, u32[]{:S(2)}) collective-permute-start(f32[144,1024]{1,0:T(8,128)S(1)} %constant_dynamic-update-slice_fusion.rest), channel_id=1, source_target_pairs={{0,8},{1,9},{2,10},{3,11},{4,12},{5,13},{6,14},{7,15},{8,16},{9,17... | collective-permute-start | bytes 1769480 | tf_op jit(solution)/shard_map/ppermute | solution.py:48
  51.3 13.2 %collective-permute-start.13 = (f32[144,1024]{1,0:T(8,128)S(1)}, f32[144,1024]{1,0:T(8,128)S(1)}, u32[]{:S(2)}, u32[]{:S(2)}) collective-permute-start(f32[144,1024]{1,0:T(8,128)S(1)} %collective-permute-done.4.refs_1_), channel_id=1, source_target_pairs={{0,1},{1,0},{2,3},{3,2},{4,5},{5,4},{6,7},{7,6},{8,9},{9,8},{10,11... | collective-permute-start | bytes 1769480 | tf_op jit(solution)/shard_map/ppermute | solution.py:48
  53.8 10.8 %collective-permute-start.14 = (f32[144,1024]{1,0:T(8,128)S(1)}, f32[144,1024]{1,0:T(8,128)S(1)}, u32[]{:S(2)}, u32[]{:S(2)}) collective-permute-start(f32[144,1024]{1,0:T(8,128)S(1)} %collective-permute-done.5.refs_2_), channel_id=1, source_target_pairs={{0,1},{1,0},{2,3},{3,2},{4,5},{5,4},{6,7},{7,6},{8,9},{9,8},{10,11... | collective-permute-start | bytes 1769480 | tf_op jit(solution)/shard_map/ppermute | solution.py:48
  55.1 17.3 %collective-permute-start.11 = (f32[96,1024]{1,0:T(8,128)}, f32[96,1024]{1,0:T(8,128)}, u32[]{:S(2)}, u32[]{:S(2)}) collective-permute-start(f32[96,1024]{1,0:T(8,128)} %slice.7), channel_id=1, source_target_pairs={{0,24},{1,25},{2,26},{3,27},{4,28},{5,29},{6,30},{7,31},{8,0},{9,1... | collective-permute-start | bytes 1179656 | tf_op jit(solution)/shard_map/ppermute | solution.py:48
  59.3 13.1 %collective-permute-start.10 = (f32[96,1024]{1,0:T(8,128)}, f32[96,1024]{1,0:T(8,128)}, u32[]{:S(2)}, u32[]{:S(2)}) collective-permute-start(f32[96,1024]{1,0:T(8,128)} %pad_maximum_fusion.3), channel_id=1, source_target_pairs={{0,8},{1,9},{2,10},{3,11},{4,12},{5,13},{6,14},{7,15},{8,16},{9,17... | collective-permute-start | bytes 1179656 | tf_op jit(solution)/shard_map/ppermute | solution.py:48
  59.3 23.3 %collective-permute-start.15 = (f32[96,1024]{1,0:T(8,128)S(1)}, f32[96,1024]{1,0:T(8,128)S(1)}, u32[]{:S(2)}, u32[]{:S(2)}) collective-permute-start(f32[96,1024]{1,0:T(8,128)S(1)} %constant_dynamic-slice_fusion), channel_id=1, source_target_pairs={{0,128},{1,129},{2,130},{3,131},{4,132},{5,133},{6,134},{7,135},{8... | collective-permute-start | bytes 1179656 | tf_op jit(solution)/shard_map/ppermute | solution.py:48
  72.4 10.3 %collective-permute-start.16 = (f32[96,1024]{1,0:T(8,128)}, f32[96,1024]{1,0:T(8,128)S(1)}, u32[]{:S(2)}, u32[]{:S(2)}) collective-permute-start(f32[96,1024]{1,0:T(8,128)} %collective-permute-done.10.refs_6_), channel_id=1, source_target_pairs={{0,1},{1,0},{2,3},{3,2},{4,5},{5,4},{6,7},{7,6},{8,9},{9,8},{10,11... | collective-permute-start | bytes 1179656 | tf_op jit(solution)/shard_map/ppermute | solution.py:48
  96.5 14.9 %collective-permute-start.21 = (f32[576,128]{1,0:T(8,128)S(1)}, f32[576,128]{1,0:T(8,128)S(1)}, u32[]{:S(2)}, u32[]{:S(2)}) collective-permute-start(f32[576,128]{1,0:T(8,128)S(1)} %get-tuple-element.48), channel_id=1, source_target_pairs={{0,24},{1,25},{2,26},{3,27},{4,28},{5,29},{6,30},{7,31},{8,0},{9,1... | collective-permute-start | bytes 884744 | tf_op jit(solution)/shard_map/ppermute | solution.py:48
  99.2 12.2 %collective-permute-start.20 = (f32[576,128]{1,0:T(8,128)S(1)}, f32[576,128]{1,0:T(8,128)S(1)}, u32[]{:S(2)}, u32[]{:S(2)}) collective-permute-start(f32[576,128]{1,0:T(8,128)S(1)} %get-tuple-element.49), channel_id=1, source_target_pairs={{0,16},{1,17},{2,18},{3,19},{4,20},{5,21},{6,22},{7,23},{8,24},{9,... | collective-permute-start | bytes 884744 | tf_op jit(solution)/shard_map/ppermute | solution.py:48
  99.2 16.2 %collective-permute-start.19 = (f32[576,128]{1,0:T(8,128)S(1)}, f32[576,128]{1,0:T(8,128)S(1)}, u32[]{:S(2)}, u32[]{:S(2)}) collective-permute-start(f32[576,128]{1,0:T(8,128)S(1)} %get-tuple-element.50), channel_id=1, source_target_pairs={{0,8},{1,9},{2,10},{3,11},{4,12},{5,13},{6,14},{7,15},{8,16},{9,17... | collective-permute-start | bytes 884744 | tf_op jit(solution)/shard_map/ppermute | solution.py:48
  123.1 23.9 %collective-permute-start.38 = (f32[2,48,1024]{2,1,0:T(8,128)S(1)}, f32[2,48,1024]{2,1,0:T(8,128)S(1)}, u32[]{:S(2)}, u32[]{:S(2)}) collective-permute-start(f32[2,48,1024]{2,1,0:T(8,128)S(1)} %copy-done.23), channel_id=1, source_target_pairs={{0,32},{1,33},{2,34},{3,35},{4,36},{5,37},{6,38},{7,39},{8,40},{9,... | collective-permute-start | bytes 1179656 | tf_op jit(solution)/shard_map/ppermute | solution.py:48
  144.7 23.1 %collective-permute-start.40 = (f32[2,48,1024]{2,1,0:T(8,128)S(1)}, f32[2,48,1024]{2,1,0:T(8,128)S(1)}, u32[]{:S(2)}, u32[]{:S(2)}) collective-permute-start(f32[2,48,1024]{2,1,0:T(8,128)S(1)} %copy-done.21), channel_id=1, source_target_pairs={{0,96},{1,97},{2,98},{3,99},{4,100},{5,101},{6,102},{7,103},{8,104... | collective-permute-start | bytes 1179656 | tf_op jit(solution)/shard_map/ppermute | solution.py:48
  146.5 11.9 %collective-permute-start.33 = (f32[576,128]{1,0:T(8,128)S(1)}, f32[576,128]{1,0:T(8,128)S(1)}, u32[]{:S(2)}, u32[]{:S(2)}) collective-permute-start(f32[576,128]{1,0:T(8,128)S(1)} %pad_maximum_fusion.4.refs_0_), channel_id=1, source_target_pairs={{0,24},{1,25},{2,26},{3,27},{4,28},{5,29},{6,30},{7,31},{8,0},{9,1... | collective-permute-start | bytes 884744 | tf_op jit(solution)/shard_map/ppermute | solution.py:48
  146.7 16.4 %collective-permute-start.32 = (f32[576,128]{1,0:T(8,128)S(1)}, f32[576,128]{1,0:T(8,128)S(1)}, u32[]{:S(2)}, u32[]{:S(2)}) collective-permute-start(f32[576,128]{1,0:T(8,128)S(1)} %pad_maximum_fusion.4.refs_0_), channel_id=1, source_target_pairs={{0,16},{1,17},{2,18},{3,19},{4,20},{5,21},{6,22},{7,23},{8,24},{9,... | collective-permute-start | bytes 884744 | tf_op jit(solution)/shard_map/ppermute | solution.py:48
  147.0 17.8 %collective-permute-start.31 = (f32[576,128]{1,0:T(8,128)S(1)}, f32[576,128]{1,0:T(8,128)S(1)}, u32[]{:S(2)}, u32[]{:S(2)}) collective-permute-start(f32[576,128]{1,0:T(8,128)S(1)} %pad_maximum_fusion.4.refs_0_), channel_id=1, source_target_pairs={{0,8},{1,9},{2,10},{3,11},{4,12},{5,13},{6,14},{7,15},{8,16},{9,17... | collective-permute-start | bytes 884744 | tf_op jit(solution)/shard_map/ppermute | solution.py:48
  150.7 34.3 %collective-permute-start.34 = (f32[576,128]{1,0:T(8,128)S(1)}, f32[576,128]{1,0:T(8,128)S(1)}, u32[]{:S(2)}, u32[]{:S(2)}) collective-permute-start(f32[576,128]{1,0:T(8,128)S(1)} %pad_maximum_fusion.4.refs_0_), channel_id=1, source_target_pairs={{0,1},{1,0},{2,3},{3,2},{4,5},{5,4},{6,7},{7,6},{8,9},{9,8},{10,11... | collective-permute-start | bytes 884744 | tf_op jit(solution)/shard_map/ppermute | solution.py:48
  158.4 26.6 %collective-permute-start.37 = (f32[576,128]{1,0:T(8,128)S(1)}, f32[576,128]{1,0:T(8,128)S(1)}, u32[]{:S(2)}, u32[]{:S(2)}) collective-permute-start(f32[576,128]{1,0:T(8,128)S(1)} %collective-permute-done.33.refs_3_), channel_id=1, source_target_pairs={{0,1},{1,0},{2,3},{3,2},{4,5},{5,4},{6,7},{7,6},{8,9},{9,8},{10,11... | collective-permute-start | bytes 884744 | tf_op jit(solution)/shard_map/ppermute | solution.py:48
  163.0 22.0 %collective-permute-start.36 = (f32[576,128]{1,0:T(8,128)S(1)}, f32[576,128]{1,0:T(8,128)S(1)}, u32[]{:S(2)}, u32[]{:S(2)}) collective-permute-start(f32[576,128]{1,0:T(8,128)S(1)} %collective-permute-done.32.refs_2_), channel_id=1, source_target_pairs={{0,1},{1,0},{2,3},{3,2},{4,5},{5,4},{6,7},{7,6},{8,9},{9,8},{10,11... | collective-permute-start | bytes 884744 | tf_op jit(solution)/shard_map/ppermute | solution.py:48
  164.8 20.3 %collective-permute-start.35 = (f32[576,128]{1,0:T(8,128)S(1)}, f32[576,128]{1,0:T(8,128)S(1)}, u32[]{:S(2)}, u32[]{:S(2)}) collective-permute-start(f32[576,128]{1,0:T(8,128)S(1)} %collective-permute-done.31.refs_1_), channel_id=1, source_target_pairs={{0,1},{1,0},{2,3},{3,2},{4,5},{5,4},{6,7},{7,6},{8,9},{9,8},{10,11... | collective-permute-start | bytes 884744 | tf_op jit(solution)/shard_map/ppermute | solution.py:48
  170.7 14.3 %collective-permute-start.41 = (f32[48,1024]{1,0:T(8,128)}, f32[48,1024]{1,0:T(8,128)S(1)}, u32[]{:S(2)}, u32[]{:S(2)}) collective-permute-start(f32[48,1024]{1,0:T(8,128)} %get-tuple-element.45), channel_id=1, source_target_pairs={{0,128},{1,129},{2,130},{3,131},{4,132},{5,133},{6,134},{7,135},{8... | collective-permute-start | bytes 589832 | tf_op jit(solution)/shard_map/ppermute | solution.py:48
  (45 other events, 408.9 us)
where the time goes:
time: 191 us
  waiting for transfers between devices  71.7 us (38%)
  starting transfers between devices  70.2 us (37%)
  Pallas kernels  37.9 us (20%)
  local copies, waits for them, and re-layouts  5.75 us (3%)
  other arithmetic  4.16 us (2%)
    ppermute x42, waiting for transfers between devices, sent(): return lax.ppermute(value, BOTH, perm)  71.7 us
    ppermute x42, starting transfers between devices, sent(): return lax.ppermute(value, BOTH, perm)  70.2 us
    pallas_call x7, Pallas kernels, kernel(): pl.pallas_call(body, out_shape=jax.ShapeDtypeStruct(out_shapes, F32) if s...  37.9 us
    unnamed x56, local copies, waits for them, and re-layouts  4.91 us
  transfers between devices with their start and end apart: 42, of which 19 were waited for; matrix products, arithmetic and copies ran while one was open for 1% of the time, Pallas kernels for 12%

commit v1 on v0

--- a/solution.py
+++ b/solution.py
@@ -248,8 +248,19 @@
 
 def final_kernel(*refs):
     pieces, (keep, got, base) = refs[:8], refs[8:11]
-    columns, pair_out, diag_out, whole = refs[11:]
+    columns_out, pair_out, diag_out, whole, columns, pairs, diags, done = refs[11:]
     at = place()
+    copies = []
+
+    def write(source, target):
+        copy = pltpu.make_async_copy(source, target, done.at[len(copies)])
+        copy.start()
+        copies.append(copy)
+
+    for j in range(NSUP):
+        cols = slice(j * W, (j + 1) * W)
+        columns[j] = -(keep[:, cols] + got[:, cols])
+    write(columns, columns_out)
     rows = pieces[0].shape[0]
     small = rows // 4
     for i, piece in enumerate(pieces):
@@ -258,25 +269,27 @@
             dst = pl.multiple_of(((at["y"] - k) & 3) * rows + ((at["x"] - r) & 3) * small, 8)
             whole[at["c"] ^ par, pl.ds(dst, small), :] = piece[r * small : (r + 1) * small, :]
     left, right = slice(0, HALF), slice(HALF, W)
-    for p in range(len(PAIRS)):
-        span = slice(p * W, (p + 1) * W)
-        pair_out[p, :, left] = whole[0, span, :] + base[span, left]
-        pair_out[p, :, right] = whole[1, span, :] + base[span, right]
     for t in range(2):
         full = slice(DIAG + t * W, DIAG + (t + 1) * W)
         quarter = slice(DIAG + 2 * W + t * HALF, DIAG + 2 * W + (t + 1) * HALF)
         upper, lower = (base.at[DIAG + s * W : DIAG + (s + 1) * W, :] for s in (t, t + 2))
         side = whole[0, full, :]
-        diag_out[t, :, left] = side + upper[:, left]
-        diag_out[t, :HALF, right] = side[HALF:, :].T + upper[:HALF, right]
-        diag_out[t, HALF:, right] = whole[1, quarter, :] + upper[HALF:, right]
+        diags[t, :, left] = side + upper[:, left]
+        diags[t, :HALF, right] = side[HALF:, :].T + upper[:HALF, right]
+        diags[t, HALF:, right] = whole[1, quarter, :] + upper[HALF:, right]
+        write(diags.at[t], diag_out.at[t])
         side = whole[1, full, :]
-        diag_out[t + 2, :, right] = side + lower[:, right]
-        diag_out[t + 2, HALF:, left] = side[:HALF, :].T + lower[HALF:, left]
-        diag_out[t + 2, :HALF, left] = whole[0, quarter, :] + lower[:HALF, left]
-    for j in range(NSUP):
-        cols = slice(j * W, (j + 1) * W)
-        columns[j] = -(keep[:, cols] + got[:, cols])
+        diags[t + 2, :, right] = side + lower[:, right]
+        diags[t + 2, HALF:, left] = side[:HALF, :].T + lower[HALF:, left]
+        diags[t + 2, :HALF, left] = whole[0, quarter, :] + lower[:HALF, left]
+        write(diags.at[t + 2], diag_out.at[t + 2])
+    for p in range(len(PAIRS)):
+        span = slice(p * W, (p + 1) * W)
+        pairs[p, :, left] = whole[0, span, :] + base[span, left]
+        pairs[p, :, right] = whole[1, span, :] + base[span, right]
+        write(pairs.at[p], pair_out.at[p])
+    for copy in copies:
+        copy.wait()
 
 
 def kernel(body, args, out_shapes, scratch=(), smem=0, flops=0):
@@ -346,6 +359,8 @@
     both = jnp.concatenate(firsts, axis=0)
     cross, both = tie(jnp.concatenate(cross, axis=0), both)
 
+    both2 = moved(both, "c", 1)
+
     left, right = moved(rest, "y", 1), moved(rest, "y", 3)
     distant = moved(lax.dynamic_slice_in_dim(cross, (1 - at["zh"]) * RW, 2 * RW, 0), "zh", 1)
     twin = moved(jnp.concatenate([own, rest], axis=0), "c", 1)
@@ -359,7 +374,6 @@
     left, right, start = tie(left, right, start)
     far_a = moved(jnp.concatenate([firsts[0], left[:RW]], axis=0), "y", 1)
     far_b = moved(right[RW:], "y", 3)
-    both2 = moved(both, "c", 1)
     left2, right2 = moved(left, "c", 1), moved(right, "c", 1)
     early = kernel(
         early_kernel,
@@ -396,12 +410,17 @@
     total = jnp.concatenate(lines, axis=0)
     lanes = gathered(total, "y")
     twins = [moved(v, "c", 1) for v in lanes]
-    return kernel(
+    inputs = lanes + twins + [keep, summed, base]
+    outs = [(NSUP, RW, W), (len(PAIRS), W, W), (NSUP, W, W)]
+    return pl.pallas_call(
         final_kernel,
-        lanes + twins + [keep, summed, base],
-        [(NSUP, RW, W), (len(PAIRS), W, W), (NSUP, W, W)],
-        [((2, TALL, HALF), F32)],
-    )
+        out_shape=[jax.ShapeDtypeStruct(s, F32) for s in outs],
+        in_specs=[VMEM] * len(inputs),
+        out_specs=[pl.BlockSpec(memory_space=pl.ANY)] * 3,
+        scratch_shapes=[pltpu.VMEM(s, F32) for s in [(2, TALL, HALF)] + outs]
+        + [pltpu.SemaphoreType.DMA((1 + len(ALL_BLOCKS),))],
+        compiler_params=pltpu.CompilerParams(vmem_limit_bytes=56 << 20),
+    )(*inputs)
 
 
 def solution(mesh):

time: 191 us -> 191 us (level)
    pallas_call x7 -> x6, Pallas kernels: 37.9 us -> 33.3 us  [kernel(): pl.pallas_call(body, out_shape=jax.ShapeDtypeStruct(out_shapes, F32) if s...]
    pallas_call x0 -> x1, Pallas kernels: none -> 4.44 us  [shards(): pl.pallas_call(final_kernel, out_shape=[jax.ShapeDtypeStruct(s, F32) for...]
where the time goes in v1:
time: 191 us
  waiting for transfers between devices  71.7 us (38%)
  starting transfers between devices  70.2 us (37%)
  Pallas kernels  37.8 us (20%)
  local copies, waits for them, and re-layouts  5.75 us (3%)
  other arithmetic  4.16 us (2%)
    ppermute x42, waiting for transfers between devices, sent(): return lax.ppermute(value, BOTH, perm)  71.7 us
    ppermute x42, starting transfers between devices, sent(): return lax.ppermute(value, BOTH, perm)  70.2 us
    pallas_call x6, Pallas kernels, kernel(): pl.pallas_call(body, out_shape=jax.ShapeDtypeStruct(out_shapes, F32) if s...  33.3 us
    unnamed x56, local copies, waits for them, and re-layouts  4.91 us
    pallas_call x1, Pallas kernels, shards(): pl.pallas_call(final_kernel, out_shape=[jax.ShapeDtypeStruct(s, F32) for...  4.44 us
  transfers between devices with their start and end apart: 42, of which 19 were waited for; matrix products, arithmetic and copies ran while one was open for 1% of the time, Pallas kernels for 12%

profile of v1, /device:TPU:65, one launch (start us, length us, event | category | flops | bytes accessed | tf_op | source)
XLA Modules:
  0.0 190.7 jit_solution(3330946954955420560)
XLA Ops:
  3.5 3.7 %collective-permute-start.2 = (f32[48,1024]{1,0:T(8,128)}, f32[48,1024]{1,0:T(8,128)S(1)}, u32[]{:S(2)}, u32[]{:S(2)}) collective-permute-start(f32[48,1024]{1,0:T(8,128)} %shard_map.94.own), channel_id=1, source_target_pairs={{0,4},{1,5},{2,6},{3,7},{4,0},{5,1},{6,2},{7,3},{8,12},{9,13},{10,... | collective-permute-start | bytes 589832 | tf_op jit(solution)/shard_map/ppermute | solution.py:48
  10.0 10.6 %collective-permute-done.2 = f32[48,1024]{1,0:T(8,128)S(1)} collective-permute-done((f32[48,1024]{1,0:T(8,128)}, f32[48,1024]{1,0:T(8,128)S(1)}, u32[]{:S(2)}, u32[]{:S(2)}) %collective-permute-start.2) | collective-permute-done | bytes 196640 | tf_op jit(solution)/shard_map/ppermute | solution.py:48
  20.6 3.1 %collective-permute-done.1 = f32[48,1024]{1,0:T(8,128)S(1)} collective-permute-done((f32[48,1024]{1,0:T(8,128)}, f32[48,1024]{1,0:T(8,128)S(1)}, u32[]{:S(2)}, u32[]{:S(2)}) %collective-permute-start.1) | collective-permute-done | bytes 196640 | tf_op jit(solution)/shard_map/ppermute | solution.py:48
  39.5 4.3 %collective-permute-done.7 = f32[48,1024]{1,0:T(8,128)S(1)} collective-permute-done((f32[48,1024]{1,0:T(8,128)S(1)}, f32[48,1024]{1,0:T(8,128)S(1)}, u32[]{:S(2)}, u32[]{:S(2)}) %collective-permute-start.7) | collective-permute-done | bytes 196640 | tf_op jit(solution)/shard_map/ppermute | solution.py:48
  45.5 5.7 %shard_map.95 = (f32[384,1024]{1,0:T(8,128)}, bf16[384,1536]{1,0:T(8,128)(2,1)}, bf16[384,1536]{1,0:T(8,128)(2,1)}, bf16[144,1024]{1,0:T(8,128)(2,1)}, bf16[144,1024]{1,0:T(8,128)(2,1)}) custom-call(f32[384,1536]{1,0:T(8,128)} %bitcast.1, f32[48,1024]{1,0:T(8,128)} %shard_map.94.own, f32[144,1024]{1,0:T(8,128)} %copy-done.19, f32[192,1024]{1,0:T(8,128)} %copy-done.20, ...), custom_call_target="tpu_custom_call" | custom-call | flops 2147483648 | bytes 4521984 | tf_op jit(solution)/shard_map/pallas_call | solution.py:297
  55.1 3.4 %collective-permute-start.11 = (f32[96,1024]{1,0:T(8,128)}, f32[96,1024]{1,0:T(8,128)}, u32[]{:S(2)}, u32[]{:S(2)}) collective-permute-start(f32[96,1024]{1,0:T(8,128)} %slice.7), channel_id=1, source_target_pairs={{0,24},{1,25},{2,26},{3,27},{4,28},{5,29},{6,30},{7,31},{8,0},{9,1... | collective-permute-start | bytes 1179656 | tf_op jit(solution)/shard_map/ppermute | solution.py:48
  59.3 5.2 %collective-permute-start.15 = (f32[96,1024]{1,0:T(8,128)S(1)}, f32[96,1024]{1,0:T(8,128)S(1)}, u32[]{:S(2)}, u32[]{:S(2)}) collective-permute-start(f32[96,1024]{1,0:T(8,128)S(1)} %constant_dynamic-slice_fusion), channel_id=1, source_target_pairs={{0,128},{1,129},{2,130},{3,131},{4,132},{5,133},{6,134},{7,135},{8... | collective-permute-start | bytes 1179656 | tf_op jit(solution)/shard_map/ppermute | solution.py:48
  65.7 6.7 %shard_map.96.refs_0_ = f32[384,1024]{1,0:T(8,128)} custom-call(f32[384,1024]{1,0:T(8,128)} %get-tuple-element.29.start, bf16[384,1536]{1,0:T(8,128)(2,1)} %get-tuple-element.30.ltop.refs_1_, bf16[384,1536]{1,0:T(8,128)(2,1)} %get-tuple-element.31.lbot.refs_2_, f32[96,1024]{1,0:T(8,128)} %copy-done.3, f32[144,1024]{1,0:T(8,128)} %copy-done.5, ...), custom_call_target="tpu_custom_call" | custom-call | flops 2147483648 | bytes 9437184 | tf_op jit(solution)/shard_map/pallas_call | solution.py:297
  73.2 9.5 %collective-permute-done.15.refs_5_ = f32[96,1024]{1,0:T(8,128)S(1)} collective-permute-done((f32[96,1024]{1,0:T(8,128)S(1)}, f32[96,1024]{1,0:T(8,128)S(1)}, u32[]{:S(2)}, u32[]{:S(2)}) %collective-permute-start.15) | collective-permute-done | bytes 393248 | tf_op jit(solution)/shard_map/ppermute | solution.py:48
  83.7 8.1 %shard_map.97 = (f32[2,48,1024]{2,1,0:T(8,128)}, f32[2,48,1024]{2,1,0:T(8,128)}, f32[2,48,1024]{2,1,0:T(8,128)}, f32[2,48,1024]{2,1,0:T(8,128)}, f32[2304,128]{1,0:T(8,128)}, /*index=5*/f32[2304,128]{1,0:T(8,128)}) custom-call(f32[384,1024]{1,0:T(8,128)} %shard_map.96.refs_0_, bf16[384,1536]{1,0:T(8,128)(2,1)} %get-tuple-element.30.ltop.refs_1_, ...), custom_call_target="tpu_custom_call" | custom-call | flops 4294967296 | bytes 9437184 | tf_op jit(solution)/shard_map/pallas_call | solution.py:297
  99.9 11.5 %collective-permute-done.21 = f32[576,128]{1,0:T(8,128)S(1)} collective-permute-done((f32[576,128]{1,0:T(8,128)S(1)}, f32[576,128]{1,0:T(8,128)S(1)}, u32[]{:S(2)}, u32[]{:S(2)}) %collective-permute-start.21) | collective-permute-done | bytes 294944 | tf_op jit(solution)/shard_map/ppermute | solution.py:48
  111.4 4.0 %collective-permute-done.19 = f32[576,128]{1,0:T(8,128)S(1)} collective-permute-done((f32[576,128]{1,0:T(8,128)S(1)}, f32[576,128]{1,0:T(8,128)S(1)}, u32[]{:S(2)}, u32[]{:S(2)}) %collective-permute-start.19) | collective-permute-done | bytes 294944 | tf_op jit(solution)/shard_map/ppermute | solution.py:48
  119.9 3.0 %collective-permute-done.23 = f32[144,128]{1,0:T(8,128)S(1)} collective-permute-done((f32[144,128]{1,0:T(8,128)S(1)}, f32[144,128]{1,0:T(8,128)S(1)}, u32[]{:S(2)}, u32[]{:S(2)}) %collective-permute-start.23) | collective-permute-done | bytes 73760 | tf_op jit(solution)/shard_map/ppermute | solution.py:48
  126.6 4.4 %collective-permute-done.26 = f32[144,128]{1,0:T(8,128)S(1)} collective-permute-done((f32[144,128]{1,0:T(8,128)S(1)}, f32[144,128]{1,0:T(8,128)S(1)}, u32[]{:S(2)}, u32[]{:S(2)}) %collective-permute-start.26) | collective-permute-done | bytes 73760 | tf_op jit(solution)/shard_map/ppermute | solution.py:48
  131.0 5.1 %collective-permute-start.27 = (f32[144,128]{1,0:T(8,128)S(1)}, f32[144,128]{1,0:T(8,128)S(1)}, u32[]{:S(2)}, u32[]{:S(2)}) collective-permute-start(f32[144,128]{1,0:T(8,128)S(1)} %add.174), channel_id=1, source_target_pairs={{0,128},{1,129},{2,130},{3,131},{4,132},{5,133},{6,134},{7,135},{8... | collective-permute-start | bytes 221192 | tf_op jit(solution)/shard_map/ppermute | solution.py:48
  136.0 3.6 %collective-permute-done.27 = f32[144,128]{1,0:T(8,128)S(1)} collective-permute-done((f32[144,128]{1,0:T(8,128)S(1)}, f32[144,128]{1,0:T(8,128)S(1)}, u32[]{:S(2)}, u32[]{:S(2)}) %collective-permute-start.27) | collective-permute-done | bytes 73760 | tf_op jit(solution)/shard_map/ppermute | solution.py:48
  141.7 3.1 %collective-permute-start.39 = (f32[2,48,1024]{2,1,0:T(8,128)S(1)}, f32[2,48,1024]{2,1,0:T(8,128)S(1)}, u32[]{:S(2)}, u32[]{:S(2)}) collective-permute-start(f32[2,48,1024]{2,1,0:T(8,128)S(1)} %copy-done.22), channel_id=1, source_target_pairs={{0,64},{1,65},{2,66},{3,67},{4,68},{5,69},{6,70},{7,71},{8,72},{9,... | collective-permute-start | bytes 1179656 | tf_op jit(solution)/shard_map/ppermute | solution.py:48
  150.7 7.7 %collective-permute-start.34 = (f32[576,128]{1,0:T(8,128)S(1)}, f32[576,128]{1,0:T(8,128)S(1)}, u32[]{:S(2)}, u32[]{:S(2)}) collective-permute-start(f32[576,128]{1,0:T(8,128)S(1)} %pad_maximum_fusion.4.refs_0_), channel_id=1, source_target_pairs={{0,1},{1,0},{2,3},{3,2},{4,5},{5,4},{6,7},{7,6},{8,9},{9,8},{10,11... | collective-permute-start | bytes 884744 | tf_op jit(solution)/shard_map/ppermute | solution.py:48
  158.4 4.6 %collective-permute-start.37 = (f32[576,128]{1,0:T(8,128)S(1)}, f32[576,128]{1,0:T(8,128)S(1)}, u32[]{:S(2)}, u32[]{:S(2)}) collective-permute-start(f32[576,128]{1,0:T(8,128)S(1)} %collective-permute-done.33.refs_3_), channel_id=1, source_target_pairs={{0,1},{1,0},{2,3},{3,2},{4,5},{5,4},{6,7},{7,6},{8,9},{9,8},{10,11... | collective-permute-start | bytes 884744 | tf_op jit(solution)/shard_map/ppermute | solution.py:48
  164.8 3.1 %collective-permute-start.35 = (f32[576,128]{1,0:T(8,128)S(1)}, f32[576,128]{1,0:T(8,128)S(1)}, u32[]{:S(2)}, u32[]{:S(2)}) collective-permute-start(f32[576,128]{1,0:T(8,128)S(1)} %collective-permute-done.31.refs_1_), channel_id=1, source_target_pairs={{0,1},{1,0},{2,3},{3,2},{4,5},{5,4},{6,7},{7,6},{8,9},{9,8},{10,11... | collective-permute-start | bytes 884744 | tf_op jit(solution)/shard_map/ppermute | solution.py:48
  170.7 3.1 %collective-permute-start.41 = (f32[48,1024]{1,0:T(8,128)}, f32[48,1024]{1,0:T(8,128)S(1)}, u32[]{:S(2)}, u32[]{:S(2)}) collective-permute-start(f32[48,1024]{1,0:T(8,128)} %get-tuple-element.45), channel_id=1, source_target_pairs={{0,128},{1,129},{2,130},{3,131},{4,132},{5,133},{6,134},{7,135},{8... | collective-permute-start | bytes 589832 | tf_op jit(solution)/shard_map/ppermute | solution.py:48
  173.8 7.8 %shard_map.99.refs_10_ = f32[2560,256]{1,0:T(8,128)} custom-call(s32[4]{0:T(128)} %parent.3, s32[10,3]{1,0:T(8,128)} %constant.27.clone.table, f32[6,256,256]{2,1,0:T(8,128)} %couple.2, f32[4,256,256]{2,1,0:T(8,128)} %diag_inv.1), custom_call_target="tpu_custom_call" | custom-call | flops 2147483648 | bytes 2621576 | tf_op jit(solution)/shard_map/pallas_call | solution.py:297
  181.7 3.3 %collective-permute-done.41.refs_9_ = f32[48,1024]{1,0:T(8,128)S(1)} collective-permute-done((f32[48,1024]{1,0:T(8,128)}, f32[48,1024]{1,0:T(8,128)S(1)}, u32[]{:S(2)}, u32[]{:S(2)}) %collective-permute-start.41) | collective-permute-done | bytes 196640 | tf_op jit(solution)/shard_map/ppermute | solution.py:48
  186.1 4.4 %shard_map.100 = (f32[4,48,256]{2,1,0:T(8,128)}, f32[6,256,256]{2,1,0:T(8,128)}, f32[4,256,256]{2,1,0:T(8,128)}) custom-call(f32[576,128]{1,0:T(8,128)} %copy-done.4, f32[576,128]{1,0:T(8,128)} %copy-done.13, f32[576,128]{1,0:T(8,128)} %copy-done.12, f32[576,128]{1,0:T(8,128)} %copy-done.11, f32[576,128]{1,0:T(8,128)} %copy-done.14, f32[576,128]{1,0:T(8,128)} %copy-done.17, ...), custom_call_target="tpu_custom_call" | custom-call | tf_op jit(solution)/shard_map/pallas_call | solution.py:415
  (138 shorter events, 60.7 us)
Async XLA Ops:
  3.5 17.1 %collective-permute-start.2 = (f32[48,1024]{1,0:T(8,128)}, f32[48,1024]{1,0:T(8,128)S(1)}, u32[]{:S(2)}, u32[]{:S(2)}) collective-permute-start(f32[48,1024]{1,0:T(8,128)} %shard_map.94.own), channel_id=1, source_target_pairs={{0,4},{1,5},{2,6},{3,7},{4,0},{5,1},{6,2},{7,3},{8,12},{9,13},{10,... | collective-permute-start | bytes 589832 | tf_op jit(solution)/shard_map/ppermute | solution.py:48
  7.2 16.5 %collective-permute-start.1 = (f32[48,1024]{1,0:T(8,128)}, f32[48,1024]{1,0:T(8,128)S(1)}, u32[]{:S(2)}, u32[]{:S(2)}) collective-permute-start(f32[48,1024]{1,0:T(8,128)} %shard_map.94.own), channel_id=1, source_target_pairs={{0,2},{1,3},{2,4},{3,5},{4,6},{5,7},{6,0},{7,1},{8,10},{9,11},{10,... | collective-permute-start | bytes 589832 | tf_op jit(solution)/shard_map/ppermute | solution.py:48
  24.6 20.0 %collective-permute-start.6 = (f32[192,1024]{1,0:T(8,128)S(1)}, f32[192,1024]{1,0:T(8,128)S(1)}, u32[]{:S(2)}, u32[]{:S(2)}) collective-permute-start(f32[192,1024]{1,0:T(8,128)S(1)} %pad_maximum_fusion), channel_id=1, source_target_pairs={{0,1},{1,0},{2,3},{3,2},{4,5},{5,4},{6,7},{7,6},{8,9},{9,8},{10,11... | collective-permute-start | bytes 2359304 | tf_op jit(solution)/shard_map/ppermute | solution.py:48
  28.9 22.3 %collective-permute-start.5 = (f32[144,1024]{1,0:T(8,128)S(1)}, f32[144,1024]{1,0:T(8,128)S(1)}, u32[]{:S(2)}, u32[]{:S(2)}) collective-permute-start(f32[144,1024]{1,0:T(8,128)S(1)} %constant_dynamic-update-slice_fusion.rest), channel_id=1, source_target_pairs={{0,24},{1,25},{2,26},{3,27},{4,28},{5,29},{6,30},{7,31},{8,0},{9,1... | collective-permute-start | bytes 1769480 | tf_op jit(solution)/shard_map/ppermute | solution.py:48
  31.7 19.6 %collective-permute-start.4 = (f32[144,1024]{1,0:T(8,128)S(1)}, f32[144,1024]{1,0:T(8,128)S(1)}, u32[]{:S(2)}, u32[]{:S(2)}) collective-permute-start(f32[144,1024]{1,0:T(8,128)S(1)} %constant_dynamic-update-slice_fusion.rest), channel_id=1, source_target_pairs={{0,8},{1,9},{2,10},{3,11},{4,12},{5,13},{6,14},{7,15},{8,16},{9,17... | collective-permute-start | bytes 1769480 | tf_op jit(solution)/shard_map/ppermute | solution.py:48
  51.3 13.2 %collective-permute-start.13 = (f32[144,1024]{1,0:T(8,128)S(1)}, f32[144,1024]{1,0:T(8,128)S(1)}, u32[]{:S(2)}, u32[]{:S(2)}) collective-permute-start(f32[144,1024]{1,0:T(8,128)S(1)} %collective-permute-done.4.refs_1_), channel_id=1, source_target_pairs={{0,1},{1,0},{2,3},{3,2},{4,5},{5,4},{6,7},{7,6},{8,9},{9,8},{10,11... | collective-permute-start | bytes 1769480 | tf_op jit(solution)/shard_map/ppermute | solution.py:48
  53.8 10.8 %collective-permute-start.14 = (f32[144,1024]{1,0:T(8,128)S(1)}, f32[144,1024]{1,0:T(8,128)S(1)}, u32[]{:S(2)}, u32[]{:S(2)}) collective-permute-start(f32[144,1024]{1,0:T(8,128)S(1)} %collective-permute-done.5.refs_2_), channel_id=1, source_target_pairs={{0,1},{1,0},{2,3},{3,2},{4,5},{5,4},{6,7},{7,6},{8,9},{9,8},{10,11... | collective-permute-start | bytes 1769480 | tf_op jit(solution)/shard_map/ppermute | solution.py:48
  55.1 17.3 %collective-permute-start.11 = (f32[96,1024]{1,0:T(8,128)}, f32[96,1024]{1,0:T(8,128)}, u32[]{:S(2)}, u32[]{:S(2)}) collective-permute-start(f32[96,1024]{1,0:T(8,128)} %slice.7), channel_id=1, source_target_pairs={{0,24},{1,25},{2,26},{3,27},{4,28},{5,29},{6,30},{7,31},{8,0},{9,1... | collective-permute-start | bytes 1179656 | tf_op jit(solution)/shard_map/ppermute | solution.py:48
  59.3 13.1 %collective-permute-start.10 = (f32[96,1024]{1,0:T(8,128)}, f32[96,1024]{1,0:T(8,128)}, u32[]{:S(2)}, u32[]{:S(2)}) collective-permute-start(f32[96,1024]{1,0:T(8,128)} %pad_maximum_fusion.3), channel_id=1, source_target_pairs={{0,8},{1,9},{2,10},{3,11},{4,12},{5,13},{6,14},{7,15},{8,16},{9,17... | collective-permute-start | bytes 1179656 | tf_op jit(solution)/shard_map/ppermute | solution.py:48
  59.3 23.3 %collective-permute-start.15 = (f32[96,1024]{1,0:T(8,128)S(1)}, f32[96,1024]{1,0:T(8,128)S(1)}, u32[]{:S(2)}, u32[]{:S(2)}) collective-permute-start(f32[96,1024]{1,0:T(8,128)S(1)} %constant_dynamic-slice_fusion), channel_id=1, source_target_pairs={{0,128},{1,129},{2,130},{3,131},{4,132},{5,133},{6,134},{7,135},{8... | collective-permute-start | bytes 1179656 | tf_op jit(solution)/shard_map/ppermute | solution.py:48
  72.4 10.3 %collective-permute-start.16 = (f32[96,1024]{1,0:T(8,128)}, f32[96,1024]{1,0:T(8,128)S(1)}, u32[]{:S(2)}, u32[]{:S(2)}) collective-permute-start(f32[96,1024]{1,0:T(8,128)} %collective-permute-done.10.refs_6_), channel_id=1, source_target_pairs={{0,1},{1,0},{2,3},{3,2},{4,5},{5,4},{6,7},{7,6},{8,9},{9,8},{10,11... | collective-permute-start | bytes 1179656 | tf_op jit(solution)/shard_map/ppermute | solution.py:48
  96.5 14.9 %collective-permute-start.21 = (f32[576,128]{1,0:T(8,128)S(1)}, f32[576,128]{1,0:T(8,128)S(1)}, u32[]{:S(2)}, u32[]{:S(2)}) collective-permute-start(f32[576,128]{1,0:T(8,128)S(1)} %get-tuple-element.48), channel_id=1, source_target_pairs={{0,24},{1,25},{2,26},{3,27},{4,28},{5,29},{6,30},{7,31},{8,0},{9,1... | collective-permute-start | bytes 884744 | tf_op jit(solution)/shard_map/ppermute | solution.py:48
  99.2 12.2 %collective-permute-start.20 = (f32[576,128]{1,0:T(8,128)S(1)}, f32[576,128]{1,0:T(8,128)S(1)}, u32[]{:S(2)}, u32[]{:S(2)}) collective-permute-start(f32[576,128]{1,0:T(8,128)S(1)} %get-tuple-element.49), channel_id=1, source_target_pairs={{0,16},{1,17},{2,18},{3,19},{4,20},{5,21},{6,22},{7,23},{8,24},{9,... | collective-permute-start | bytes 884744 | tf_op jit(solution)/shard_map/ppermute | solution.py:48
  99.2 16.2 %collective-permute-start.19 = (f32[576,128]{1,0:T(8,128)S(1)}, f32[576,128]{1,0:T(8,128)S(1)}, u32[]{:S(2)}, u32[]{:S(2)}) collective-permute-start(f32[576,128]{1,0:T(8,128)S(1)} %get-tuple-element.50), channel_id=1, source_target_pairs={{0,8},{1,9},{2,10},{3,11},{4,12},{5,13},{6,14},{7,15},{8,16},{9,17... | collective-permute-start | bytes 884744 | tf_op jit(solution)/shard_map/ppermute | solution.py:48
  123.1 23.9 %collective-permute-start.38 = (f32[2,48,1024]{2,1,0:T(8,128)S(1)}, f32[2,48,1024]{2,1,0:T(8,128)S(1)}, u32[]{:S(2)}, u32[]{:S(2)}) collective-permute-start(f32[2,48,1024]{2,1,0:T(8,128)S(1)} %copy-done.23), channel_id=1, source_target_pairs={{0,32},{1,33},{2,34},{3,35},{4,36},{5,37},{6,38},{7,39},{8,40},{9,... | collective-permute-start | bytes 1179656 | tf_op jit(solution)/shard_map/ppermute | solution.py:48
  144.7 23.1 %collective-permute-start.40 = (f32[2,48,1024]{2,1,0:T(8,128)S(1)}, f32[2,48,1024]{2,1,0:T(8,128)S(1)}, u32[]{:S(2)}, u32[]{:S(2)}) collective-permute-start(f32[2,48,1024]{2,1,0:T(8,128)S(1)} %copy-done.21), channel_id=1, source_target_pairs={{0,96},{1,97},{2,98},{3,99},{4,100},{5,101},{6,102},{7,103},{8,104... | collective-permute-start | bytes 1179656 | tf_op jit(solution)/shard_map/ppermute | solution.py:48
  146.5 11.9 %collective-permute-start.33 = (f32[576,128]{1,0:T(8,128)S(1)}, f32[576,128]{1,0:T(8,128)S(1)}, u32[]{:S(2)}, u32[]{:S(2)}) collective-permute-start(f32[576,128]{1,0:T(8,128)S(1)} %pad_maximum_fusion.4.refs_0_), channel_id=1, source_target_pairs={{0,24},{1,25},{2,26},{3,27},{4,28},{5,29},{6,30},{7,31},{8,0},{9,1... | collective-permute-start | bytes 884744 | tf_op jit(solution)/shard_map/ppermute | solution.py:48
  146.7 16.4 %collective-permute-start.32 = (f32[576,128]{1,0:T(8,128)S(1)}, f32[576,128]{1,0:T(8,128)S(1)}, u32[]{:S(2)}, u32[]{:S(2)}) collective-permute-start(f32[576,128]{1,0:T(8,128)S(1)} %pad_maximum_fusion.4.refs_0_), channel_id=1, source_target_pairs={{0,16},{1,17},{2,18},{3,19},{4,20},{5,21},{6,22},{7,23},{8,24},{9,... | collective-permute-start | bytes 884744 | tf_op jit(solution)/shard_map/ppermute | solution.py:48
  147.0 17.8 %collective-permute-start.31 = (f32[576,128]{1,0:T(8,128)S(1)}, f32[576,128]{1,0:T(8,128)S(1)}, u32[]{:S(2)}, u32[]{:S(2)}) collective-permute-start(f32[576,128]{1,0:T(8,128)S(1)} %pad_maximum_fusion.4.refs_0_), channel_id=1, source_target_pairs={{0,8},{1,9},{2,10},{3,11},{4,12},{5,13},{6,14},{7,15},{8,16},{9,17... | collective-permute-start | bytes 884744 | tf_op jit(solution)/shard_map/ppermute | solution.py:48
  150.7 34.3 %collective-permute-start.34 = (f32[576,128]{1,0:T(8,128)S(1)}, f32[576,128]{1,0:T(8,128)S(1)}, u32[]{:S(2)}, u32[]{:S(2)}) collective-permute-start(f32[576,128]{1,0:T(8,128)S(1)} %pad_maximum_fusion.4.refs_0_), channel_id=1, source_target_pairs={{0,1},{1,0},{2,3},{3,2},{4,5},{5,4},{6,7},{7,6},{8,9},{9,8},{10,11... | collective-permute-start | bytes 884744 | tf_op jit(solution)/shard_map/ppermute | solution.py:48
  158.4 26.6 %collective-permute-start.37 = (f32[576,128]{1,0:T(8,128)S(1)}, f32[576,128]{1,0:T(8,128)S(1)}, u32[]{:S(2)}, u32[]{:S(2)}) collective-permute-start(f32[576,128]{1,0:T(8,128)S(1)} %collective-permute-done.33.refs_3_), channel_id=1, source_target_pairs={{0,1},{1,0},{2,3},{3,2},{4,5},{5,4},{6,7},{7,6},{8,9},{9,8},{10,11... | collective-permute-start | bytes 884744 | tf_op jit(solution)/shard_map/ppermute | solution.py:48
  163.0 22.0 %collective-permute-start.36 = (f32[576,128]{1,0:T(8,128)S(1)}, f32[576,128]{1,0:T(8,128)S(1)}, u32[]{:S(2)}, u32[]{:S(2)}) collective-permute-start(f32[576,128]{1,0:T(8,128)S(1)} %collective-permute-done.32.refs_2_), channel_id=1, source_target_pairs={{0,1},{1,0},{2,3},{3,2},{4,5},{5,4},{6,7},{7,6},{8,9},{9,8},{10,11... | collective-permute-start | bytes 884744 | tf_op jit(solution)/shard_map/ppermute | solution.py:48
  164.8 20.3 %collective-permute-start.35 = (f32[576,128]{1,0:T(8,128)S(1)}, f32[576,128]{1,0:T(8,128)S(1)}, u32[]{:S(2)}, u32[]{:S(2)}) collective-permute-start(f32[576,128]{1,0:T(8,128)S(1)} %collective-permute-done.31.refs_1_), channel_id=1, source_target_pairs={{0,1},{1,0},{2,3},{3,2},{4,5},{5,4},{6,7},{7,6},{8,9},{9,8},{10,11... | collective-permute-start | bytes 884744 | tf_op jit(solution)/shard_map/ppermute | solution.py:48
  170.7 14.3 %collective-permute-start.41 = (f32[48,1024]{1,0:T(8,128)}, f32[48,1024]{1,0:T(8,128)S(1)}, u32[]{:S(2)}, u32[]{:S(2)}) collective-permute-start(f32[48,1024]{1,0:T(8,128)} %get-tuple-element.45), channel_id=1, source_target_pairs={{0,128},{1,129},{2,130},{3,131},{4,132},{5,133},{6,134},{7,135},{8... | collective-permute-start | bytes 589832 | tf_op jit(solution)/shard_map/ppermute | solution.py:48
  (45 other events, 408.9 us)
